TPU v7x, 128 devices: a whole 4x4x4 slice. The times are simulated.
128 devices in a mesh: row: 8 (over x, core), col: 16 (over y, z).
Axes of the slice: x: 4, y: 4, z: 4, core: 2. Of those that a mesh axis runs over, the one named last changes fastest.
Arguments:
- stiffness: bfloat16 [3584, 256, 256], P(('row', 'col')), may hold values from -0.25 to 0.25
- stiffness_index: int32 [3584, 2], P(('row', 'col')), may hold values from 0 to 15
- mode_basis: bfloat16 [524288, 256], P(('row', 'col')), may hold values from -0.75 to 0.75
- pair_owner: int32 [128, 2], replicated, may hold values from 0 to 1
- margin: int32 [128, 2, 4, 2], replicated, may hold values from 0 to 15
Outputs:
- coarse: bfloat16 [128, 128, 256, 256], P('row', None, 'col')
All inputs are finite; a program needn't handle non-finite values.
Results may differ from a plain program's by a relative error of at most 0.0049.
Values may be sent and summed in bfloat16 or wider, within the bound.
No kernel may reach another device: no remote copies, remote signals or barrier semaphores. Data moves between devices by JAX's collectives and lax.ppermute only.
A program may use at most 128 MiB of HBM per device.

v0:
```python
import jax
import jax.numpy as jnp
from jax import lax
from jax.sharding import PartitionSpec as P


def with_halo(array, sides, width):
    for axis, dim in sides:
        count, length = (lax.axis_size(axis), array.shape[dim])
        up = [(i, (i + 1) % count) for i in range(count - 1)]
        down = [(j, i) for i, j in up]
        last = lax.slice_in_dim(array, length - width, length, axis=dim)
        first = lax.slice_in_dim(array, 0, width, axis=dim)
        before = lax.ppermute(last, axis, up)
        after = lax.ppermute(first, axis, down)
        array = jnp.concatenate([before, array, after], axis=dim)
    return array


def from_behind(array, axis, by):
    count = lax.axis_size(axis)
    pairs = [(i, i + by) for i in range(count) if 0 <= i + by < count]
    return lax.ppermute(array, axis, pairs)


def gather_rows(blocks, picks):
    return blocks[picks].reshape(-1, blocks.shape[2])


def project(left, right):
    return jnp.einsum("nm,nk->mk", left, right, preferred_element_type=jnp.float32).astype(
        jnp.bfloat16
    )


def maybe_project(flag, left, right):
    return lax.cond(
        flag,
        lambda: project(left, right),
        lambda: jnp.zeros((left.shape[1], right.shape[1]), jnp.bfloat16),
    )


def on_device(stiffness, stiffness_index, mode_basis, pair_owner, margin):
    grid_rows = lax.axis_size("row")
    grid_cols = lax.axis_size("col")
    my_row = lax.axis_index("row")
    my_col = lax.axis_index("col")
    subdomain = my_row * grid_cols + my_col
    block_size = stiffness.shape[1]
    mode_count = mode_basis.shape[1]
    block_count = mode_basis.shape[0] // block_size
    mode_blocks = mode_basis.reshape(block_count, block_size, mode_count)
    picked = mode_blocks[stiffness_index[:, 1]]
    products = jnp.einsum("kab,kbm->kam", stiffness, picked, preferred_element_type=jnp.float32)
    selector = (stiffness_index[:, 0][None, :] == jnp.arange(block_count)[:, None]).astype(
        jnp.float32
    )
    summed = jnp.dot(
        selector, products.reshape(products.shape[0], -1), precision=lax.Precision.HIGHEST
    )
    applied = summed.astype(jnp.bfloat16).reshape(block_count, block_size, mode_count)
    diagonal = project(mode_basis, applied.reshape(-1, mode_count))
    has_next_col = my_col < grid_cols - 1
    has_prev_col = my_col > 0
    has_next_row = my_row < grid_rows - 1
    has_prev_row = my_row > 0
    prev_col = jnp.maximum(subdomain - 1, 0)
    prev_row = jnp.maximum(subdomain - grid_cols, 0)
    owner_next_col = pair_owner[subdomain, 0]
    owner_prev_col = pair_owner[prev_col, 0]
    owner_next_row = pair_owner[subdomain, 1]
    owner_prev_row = pair_owner[prev_row, 1]
    lists_next_col = margin[subdomain, 0]
    lists_prev_col = margin[prev_col, 0]
    lists_next_row = margin[subdomain, 1]
    lists_prev_row = margin[prev_row, 1]
    to_col_lower = jnp.where(owner_prev_col == 0, gather_rows(applied, lists_prev_col[:, 1]), 0)
    to_col_upper = jnp.where(owner_next_col == 1, gather_rows(applied, lists_next_col[:, 0]), 0)
    to_row_lower = jnp.where(owner_prev_row == 0, gather_rows(applied, lists_prev_row[:, 1]), 0)
    to_row_upper = jnp.where(owner_next_row == 1, gather_rows(applied, lists_next_row[:, 0]), 0)
    outgoing = jnp.stack(
        [jnp.stack([to_col_lower, to_row_lower]), jnp.stack([to_row_upper, to_col_upper])]
    )
    extended = with_halo(outgoing, (("row", 0), ("col", 1)), 1)
    from_row_lower = extended[0, 1]
    from_row_upper = extended[3, 2]
    from_col_lower = extended[2, 0]
    from_col_upper = extended[1, 3]
    own_next_col = has_next_col & (owner_next_col == 0)
    own_prev_col = has_prev_col & (owner_prev_col == 1)
    own_next_row = has_next_row & (owner_next_row == 0)
    own_prev_row = has_prev_row & (owner_prev_row == 1)
    next_col_block = maybe_project(
        own_next_col, gather_rows(mode_blocks, lists_next_col[:, 0]), from_col_upper
    )
    prev_col_block = maybe_project(
        own_prev_col, from_col_lower, gather_rows(mode_blocks, lists_prev_col[:, 1])
    )
    local_row = maybe_project(
        own_next_row, gather_rows(mode_blocks, lists_next_row[:, 0]), from_row_upper
    )
    lower_row = maybe_project(
        own_prev_row, from_row_lower, gather_rows(mode_blocks, lists_prev_row[:, 1])
    )
    returned = from_behind(lower_row, "row", -1)
    row_block = jnp.where(owner_next_row == 0, local_row, returned)
    slots = jnp.stack([diagonal, next_col_block, row_block, prev_col_block])
    row_shift = [0, 0, 0, -1]
    col_offset = [0, 1, grid_cols, 0]
    slot_count = slots.shape[0]
    part_rows = mode_count // grid_cols
    pieces = slots.reshape(slot_count, grid_cols, part_rows, mode_count)
    received = lax.all_to_all(pieces, "col", split_axis=1, concat_axis=1, tiled=True)
    sources = jnp.arange(grid_cols, dtype=jnp.int32)
    local_index = sources[None, :] + jnp.array(row_shift, jnp.int32)[:, None]
    local_index = jnp.where(local_index < 0, grid_cols, local_index)
    global_index = my_row * grid_cols + sources[None, :] + jnp.array(col_offset, jnp.int32)[:, None]
    total_subdomains = grid_rows * grid_cols
    stored = jnp.zeros((grid_cols, total_subdomains, part_rows, mode_count), jnp.bfloat16)
    return stored.at[local_index, global_index].add(received, mode="drop")


def solution(mesh):
    return jax.shard_map(
        on_device,
        mesh=mesh,
        in_specs=(
            P(("row", "col"), None, None),
            P(("row", "col"), None),
            P(("row", "col"), None),
            P(),
            P(),
        ),
        out_specs=P("row", None, "col", None),
        check_vma=False,
    )
```

profile of v0, /device:TPU:2, one launch (start us, length us, event | category | flops | bytes accessed | tf_op | source)
XLA Modules:
  0.0 166.3 jit_solution(16223815585203960740)
XLA Ops:
  4.8 4.2 %gather_fusion.4 = bf16[28,256,256]{2,1,0:T(8,128)(2,1)} fusion(bf16[16,256,256]{2,1,0:T(8,128)(2,1)} %bitcast.87, s32[1024]{0:T(1024)S(1)} %pad_clamp_fusion.8), kind=kCustom, calls=%fused_computation.4 | custom fusion | bytes 7340144 | tf_op jit(solution)/shard_map/gather | solution.py:54
  9.0 7.4 %convolution_bitcast_fusion = f32[28,256,256]{1,2,0:T(8,128)} fusion(bf16[28,256,256]{2,1,0:T(8,128)(2,1)} %gather_fusion.4, bf16[28,256,256]{2,1,0:T(8,128)(2,1)} %param.15), kind=kOutput, calls=%fused_computation.29 | convolution fusion | flops 939524096 | bytes 14680064 | tf_op jit(solution)/shard_map/kab,kbm->kam/dot_general | solution.py:55
  16.4 8.4 %copy.35 = f32[28,256,256]{2,1,0:T(8,128)} copy(f32[28,256,256]{1,2,0:T(8,128)} %convolution_bitcast_fusion) | data formatting | bytes 14680064 | tf_op jit(solution)/shard_map/kab,kbm->kam/dot_general | solution.py:55
  24.7 4.0 %pad.21 = f32[32,256,256]{2,1,0:T(8,128)S(1)} pad(f32[28,256,256]{2,1,0:T(8,128)} %copy.35, f32[]{:T(128)} %constant.110), padding=0_4x0_0x0_0 | pad | bytes 15728644
  28.7 4.9 %copy.49 = f32[4,8,256,256]{3,1,2,0:T(8,128)S(1)} copy(f32[4,8,256,256]{3,2,1,0:T(8,128)S(1)} %bitcast.84) | data formatting | bytes 16777216
  33.6 3.1 %convolution_convert_fusion.4 = bf16[16,65536]{1,0:T(8,128)(2,1)S(1)} fusion(f32[28,65536]{1,0:T(8,128)S(1)} %bitcast.85, s32[28]{0:T(128)S(1)} %get-tuple-element.82), kind=kOutput, calls=%fused_computation.27 | convolution fusion | flops 353370560 | bytes 9437296 | tf_op jit(solution)/shard_map/dot_general | solution.py:59
  38.5 2.2 %gather_fusion.6 = bf16[4,256,256]{2,1,0:T(8,128)(2,1)S(1)} fusion(bf16[16,256,256]{2,1,0:T(8,128)(2,1)} %bitcast.92, s32[1024]{0:T(1024)S(1)} %pad_clamp_fusion.6), kind=kCustom, calls=%fused_computation.6 | custom fusion | bytes 1048592 | tf_op jit(solution)/shard_map/gather | solution.py:27
  40.7 2.2 %gather_fusion.5 = bf16[4,256,256]{2,1,0:T(8,128)(2,1)S(1)} fusion(bf16[16,256,256]{2,1,0:T(8,128)(2,1)} %bitcast.93, s32[1024]{0:T(1024)S(1)} %pad_clamp_fusion.7), kind=kCustom, calls=%fused_computation.5 | custom fusion | bytes 1048592 | tf_op jit(solution)/shard_map/gather | solution.py:27
  46.4 3.0 %gather_fusion.8 = bf16[4,256,256]{2,1,0:T(8,128)(2,1)} fusion(bf16[16,256,256]{2,1,0:T(8,128)(2,1)} %bitcast.94, s32[1024]{0:T(1024)S(1)} %pad_clamp_fusion.4), kind=kCustom, calls=%fused_computation.8 | custom fusion | bytes 1048592 | tf_op jit(solution)/shard_map/gather | solution.py:27
  49.4 3.0 %gather_fusion.7 = bf16[4,256,256]{2,1,0:T(8,128)(2,1)} fusion(bf16[16,256,256]{2,1,0:T(8,128)(2,1)} %bitcast.95, s32[1024]{0:T(1024)S(1)} %pad_clamp_fusion.5), kind=kCustom, calls=%fused_computation.7 | custom fusion | bytes 1048592 | tf_op jit(solution)/shard_map/gather | solution.py:27
  53.6 3.6 %collective-permute-start.1 = (bf16[1,2,1024,256]{3,2,1,0:T(8,128)(2,1)S(1)}, bf16[1,2,1024,256]{3,2,1,0:T(8,128)(2,1)S(1)}, u32[]{:S(2)}, u32[]{:S(2)}) collective-permute-start(bf16[1,2,1024,256]{3,2,1,0:T(8,128)(2,1)S(1)} %maximum_bitcast_fusion.1), channel_id=1, source_target_pairs={{16,0},{32,16},{48,32},{64,48},{80,64},{96,80},{112,96},{17,1},{33... | collective-permute-start | bytes 3145736 | tf_op jit(solution)/shard_map/ppermute | solution.py:15
  57.2 2.1 %collective-permute-done = bf16[1,2,1024,256]{3,2,1,0:T(8,128)(2,1)} collective-permute-done((bf16[1,2,1024,256]{3,2,1,0:T(8,128)(2,1)S(1)}, bf16[1,2,1024,256]{3,2,1,0:T(8,128)(2,1)}, u32[]{:S(2)}, u32[]{:S(2)}) %collective-permute-start) | collective-permute-done | bytes 1048608 | tf_op jit(solution)/shard_map/ppermute | solution.py:14
  59.3 10.2 %collective-permute-done.1 = bf16[1,2,1024,256]{3,2,1,0:T(8,128)(2,1)S(1)} collective-permute-done((bf16[1,2,1024,256]{3,2,1,0:T(8,128)(2,1)S(1)}, bf16[1,2,1024,256]{3,2,1,0:T(8,128)(2,1)S(1)}, u32[]{:S(2)}, u32[]{:S(2)}) %collective-permute-start.1) | collective-permute-done | bytes 1048608 | tf_op jit(solution)/shard_map/ppermute | solution.py:15
  72.1 2.3 %fusion.14 = (bf16[4,1,1024,256]{3,2,1,0:T(8,128)(2,1)}, bf16[4,1,1024,256]{3,2,1,0:T(8,128)(2,1)}) fusion(bf16[4,2,1024,256]{3,2,1,0:T(8,128)(2,1)S(1)} %pad_maximum_fusion), kind=kLoop, calls=%fused_computation.72 | loop fusion | bytes 8388608 | tf_op jit(solution)/shard_map/slice | solution.py:13
  75.7 5.9 %collective-permute-start.4 = (bf16[4,1,1024,256]{3,2,1,0:T(8,128)(2,1)}, bf16[4,1,1024,256]{3,2,1,0:T(8,128)(2,1)}, u32[]{:S(2)}, u32[]{:S(2)}) collective-permute-start(bf16[4,1,1024,256]{3,2,1,0:T(8,128)(2,1)} %get-tuple-element.73), channel_id=1, source_target_pairs={{0,1},{1,2},{2,3},{3,4},{4,5},{5,6},{6,7},{7,8},{8,9},{9,10},{10,1... | collective-permute-start | bytes 6291464 | tf_op jit(solution)/shard_map/ppermute | solution.py:14
  86.2 4.0 %convolution_convert_fusion.5 = bf16[256,256]{0,1:T(8,128)(2,1)} fusion(bf16[4096,256]{1,0:T(8,128)(2,1)} %reshape_reshape.3, bf16[4096,256]{1,0:T(8,128)(2,1)} %param.17), kind=kOutput, calls=%fused_computation.30 | convolution fusion | flops 536936448 | bytes 4325376 | tf_op jit(solution)/shard_map/nm,nk->mk/dot_general | solution.py:31
  90.2 2.9 %conditional.6 = (bf16[256,256]{0,1:T(8,128)(2,1)S(1)}) conditional(s32[]{:T(128)} %convert_element_type.50, () %tuple.37, (bf16[16,256,256]{2,1,0:T(8,128)(2,1)S(1)}, s32[4,1]{0,1:T(1,128)S(1)}, bf16[1,2,1024,256]{3,2,1,0:T(8,128)(2,1)}) %tuple.60), branch_computations={%region_4.5_spmd, %region_5.6_spmd} | conditional | flops 134284288 | bytes 2232360 | solution.py:37
  93.1 3.8 %collective-permute-start.3 = (bf16[256,256]{0,1:T(8,128)(2,1)S(1)}, bf16[256,256]{0,1:T(8,128)(2,1)S(1)}, u32[]{:S(2)}, u32[]{:S(2)}) collective-permute-start(bf16[256,256]{0,1:T(8,128)(2,1)S(1)} %get-tuple-element.89), channel_id=1, source_target_pairs={{16,0},{32,16},{48,32},{64,48},{80,64},{96,80},{112,96},{17,1},{33... | collective-permute-start | bytes 393224 | tf_op jit(solution)/shard_map/ppermute | solution.py:23
  97.0 2.4 %collective-permute-done.3 = bf16[256,256]{0,1:T(8,128)(2,1)S(1)} collective-permute-done((bf16[256,256]{0,1:T(8,128)(2,1)S(1)}, bf16[256,256]{0,1:T(8,128)(2,1)S(1)}, u32[]{:S(2)}, u32[]{:S(2)}) %collective-permute-start.3) | collective-permute-done | bytes 131104 | tf_op jit(solution)/shard_map/ppermute | solution.py:23
  99.6 23.5 %collective-permute-done.2 = bf16[4,1,1024,256]{3,2,1,0:T(8,128)(2,1)} collective-permute-done((bf16[4,1,1024,256]{3,2,1,0:T(8,128)(2,1)}, bf16[4,1,1024,256]{3,2,1,0:T(8,128)(2,1)}, u32[]{:S(2)}, u32[]{:S(2)}) %collective-permute-start.2) | collective-permute-done | bytes 2097184 | tf_op jit(solution)/shard_map/ppermute | solution.py:15
  126.0 14.1 %all-to-all-start = ((bf16[4,16,16,256]{3,2,0,1:T(8,128)(2,1)}), bf16[4,16,16,256]{3,2,0,1:T(8,128)(2,1)S(1)}, u32[]{:S(2)}, u32[]{:S(2)}) async-start(bf16[4,16,16,256]{3,2,0,1:T(8,128)(2,1)} %pad_maximum_fusion.1), calls=%async_computation | async-start | bytes 1048576 | tf_op jit(solution)/shard_map/all_to_all | solution.py:114
  140.3 11.2 %all-to-all-done = bf16[4,16,16,256]{3,2,0,1:T(8,128)(2,1)S(1)} async-done(((bf16[4,16,16,256]{3,2,0,1:T(8,128)(2,1)}), bf16[4,16,16,256]{3,2,0,1:T(8,128)(2,1)S(1)}, u32[]{:S(2)}, u32[]{:S(2)}) %all-to-all-start) | async-done | bytes 524320 | tf_op jit(solution)/shard_map/all_to_all | solution.py:114
  151.5 6.0 %broadcast_in_dim.12 = bf16[16,128,16,256]{3,2,1,0:T(8,128)(2,1)} broadcast(bf16[]{:T(256)} %constant.25.clone.1), dimensions={} | broadcast | bytes 16777218 | tf_op jit(solution)/shard_map/broadcast_in_dim | solution.py:120
  157.5 8.8 %scatter_fusion = bf16[16,128,16,256]{3,2,1,0:T(8,128)(2,1)} fusion(bf16[16,128,16,256]{3,2,1,0:T(8,128)(2,1)} %broadcast_in_dim.12, s32[64]{0:T(128)S(1)} %reshape.290, bf16[64,16,256]{2,1,0:T(8,128)(2,1)S(1)} %bitcast.96), kind=kCustom, calls=%fused_computation.9 | custom fusion | flops 262144 | bytes 1573376 | tf_op jit(solution)/shard_map/scatter-add | solution.py:121
  (59 shorter events, 22.8 us)
Async XLA Ops:
  43.1 16.2 %collective-permute-start = (bf16[1,2,1024,256]{3,2,1,0:T(8,128)(2,1)S(1)}, bf16[1,2,1024,256]{3,2,1,0:T(8,128)(2,1)}, u32[]{:S(2)}, u32[]{:S(2)}) collective-permute-start(bf16[1,2,1024,256]{3,2,1,0:T(8,128)(2,1)S(1)} %maximum_bitcast_fusion), channel_id=1, source_target_pairs={{0,16},{16,32},{32,48},{48,64},{64,80},{80,96},{96,112},{1,17},{17... | collective-permute-start | bytes 3145736 | tf_op jit(solution)/shard_map/ppermute | solution.py:14
  53.6 15.9 %collective-permute-start.1 = (bf16[1,2,1024,256]{3,2,1,0:T(8,128)(2,1)S(1)}, bf16[1,2,1024,256]{3,2,1,0:T(8,128)(2,1)S(1)}, u32[]{:S(2)}, u32[]{:S(2)}) collective-permute-start(bf16[1,2,1024,256]{3,2,1,0:T(8,128)(2,1)S(1)} %maximum_bitcast_fusion.1), channel_id=1, source_target_pairs={{16,0},{32,16},{48,32},{64,48},{80,64},{96,80},{112,96},{17,1},{33... | collective-permute-start | bytes 3145736 | tf_op jit(solution)/shard_map/ppermute | solution.py:15
  69.5 1.0 copy-start.1
  74.4 48.7 %collective-permute-start.2 = (bf16[4,1,1024,256]{3,2,1,0:T(8,128)(2,1)}, bf16[4,1,1024,256]{3,2,1,0:T(8,128)(2,1)}, u32[]{:S(2)}, u32[]{:S(2)}) collective-permute-start(bf16[4,1,1024,256]{3,2,1,0:T(8,128)(2,1)} %get-tuple-element.72), channel_id=1, source_target_pairs={{1,0},{2,1},{3,2},{4,3},{5,4},{6,5},{7,6},{8,7},{9,8},{10,9},{11,1... | collective-permute-start | bytes 6291464 | tf_op jit(solution)/shard_map/ppermute | solution.py:15
  75.7 49.4 %collective-permute-start.4 = (bf16[4,1,1024,256]{3,2,1,0:T(8,128)(2,1)}, bf16[4,1,1024,256]{3,2,1,0:T(8,128)(2,1)}, u32[]{:S(2)}, u32[]{:S(2)}) collective-permute-start(bf16[4,1,1024,256]{3,2,1,0:T(8,128)(2,1)} %get-tuple-element.73), channel_id=1, source_target_pairs={{0,1},{1,2},{2,3},{3,4},{4,5},{5,6},{6,7},{7,8},{8,9},{9,10},{10,1... | collective-permute-start | bytes 6291464 | tf_op jit(solution)/shard_map/ppermute | solution.py:14
  86.2 4.0 %copy-start = (bf16[4096,256]{1,0:T(8,128)(2,1)S(1)}, bf16[4096,256]{1,0:T(8,128)(2,1)}, u32[]{:S(2)}) copy-start(bf16[4096,256]{1,0:T(8,128)(2,1)} %param.17) | copy-start | bytes 6291460
  86.2 10.8 %copy-start.2 = (bf16[1,2,1024,256]{3,2,1,0:T(8,128)(2,1)S(1)}, bf16[1,2,1024,256]{3,2,1,0:T(8,128)(2,1)}, u32[]{:S(2)}) copy-start(bf16[1,2,1024,256]{3,2,1,0:T(8,128)(2,1)} %copy-done.1) | copy-start | bytes 3145732
  93.1 6.3 %collective-permute-start.3 = (bf16[256,256]{0,1:T(8,128)(2,1)S(1)}, bf16[256,256]{0,1:T(8,128)(2,1)S(1)}, u32[]{:S(2)}, u32[]{:S(2)}) collective-permute-start(bf16[256,256]{0,1:T(8,128)(2,1)S(1)} %get-tuple-element.89), channel_id=1, source_target_pairs={{16,0},{32,16},{48,32},{64,48},{80,64},{96,80},{112,96},{17,1},{33... | collective-permute-start | bytes 393224 | tf_op jit(solution)/shard_map/ppermute | solution.py:23
  97.0 28.1 %copy-start.3 = (bf16[256,256]{0,1:T(8,128)(2,1)S(1)}, bf16[256,256]{0,1:T(8,128)(2,1)}, u32[]{:S(2)}) copy-start(bf16[256,256]{0,1:T(8,128)(2,1)} %convolution_convert_fusion.5) | copy-start | bytes 393220
  123.1 17.0 %copy-start.4 = (s32[4]{0:T(128)S(1)}, s32[4]{0:T(128)}, u32[]{:S(2)}) copy-start(s32[4]{0:T(128)} %constant.60.clone) | copy-start | bytes 52
  123.1 17.0 %copy-start.5 = (s32[4]{0:T(128)S(1)}, s32[4]{0:T(128)}, u32[]{:S(2)}) copy-start(s32[4]{0:T(128)} %constant.59.clone) | copy-start | bytes 52
  126.0 25.5 %all-to-all-start = ((bf16[4,16,16,256]{3,2,0,1:T(8,128)(2,1)}), bf16[4,16,16,256]{3,2,0,1:T(8,128)(2,1)S(1)}, u32[]{:S(2)}, u32[]{:S(2)}) async-start(bf16[4,16,16,256]{3,2,0,1:T(8,128)(2,1)} %pad_maximum_fusion.1), calls=%async_computation | async-start | bytes 1048576 | tf_op jit(solution)/shard_map/all_to_all | solution.py:114
where the time goes:
time: 167 us; the launch traced here: 166 us
  local copies, waits for them, and re-layouts  49.8 us (30%)
  waiting for transfers between devices  49.4 us (30%)
  starting transfers between devices  30.6 us (18%)
  matrix products  17.4 us (10%)
  other arithmetic  13.6 us (8%)
  between operations  5.43 us (3%)
    ppermute x2, waiting for transfers between devices, with_halo(): after = lax.ppermute(first, axis, down)  33.8 us
    all_to_all x1, starting transfers between devices, on_device(): lax.all_to_all(pieces, 'col', split_axis=1, concat_axis=1, tiled=True)  14.1 us
    gather x6, local copies, waits for them, and re-layouts, gather_rows(): return blocks[picks].reshape(-1, blocks.shape[2])  12.2 us
    unnamed x15, local copies, waits for them, and re-layouts  11.7 us
    all_to_all x1, waiting for transfers between devices, on_device(): lax.all_to_all(pieces, 'col', split_axis=1, concat_axis=1, tiled=True)  11.2 us
    scatter-add x1, other arithmetic, on_device(): return stored.at[local_index, global_index].add(received, mode='drop')  8.77 us
    dot_general x1, local copies, waits for them, and re-layouts, on_device(): jnp.einsum('kab,kbm->kam', stiffness, picked, preferred_element_type=jnp....  8.36 us
    ppermute x2, starting transfers between devices, with_halo(): before = lax.ppermute(last, axis, up)  7.77 us
  transfers between devices with their start and end apart: 6, of which 5 were waited for; matrix products, arithmetic and copies ran while one was open for 11% of the time, Pallas kernels for 0%

commit v1 on v0

v1 whole, which is shorter than its diff:
```python
import functools

import jax
import jax.numpy as jnp
from jax import lax
from jax.experimental import pallas as pl
from jax.experimental.pallas import tpu as pltpu
from jax.sharding import PartitionSpec as P

F32 = jnp.float32
BF16 = jnp.bfloat16
ANY = pl.BlockSpec(memory_space=pl.ANY)
VMEM = pl.BlockSpec(memory_space=pltpu.VMEM)
SMEM = pl.BlockSpec(memory_space=pltpu.SMEM)


def place():
    row = lax.axis_index("row")
    col = lax.axis_index("col")
    sub = row * lax.axis_size("col") + col
    return row, col, sub, lax.rem(row, 2)


def side_block(owners, lists, direction, first, side, j):
    use_applied = owners[direction, first] + side == 1
    return lists[direction, j, side, first], use_applied


def sides(sub, odd, cols):
    before = jnp.maximum(sub - 1, 0)
    above = jnp.maximum(sub - cols, 0)
    send_col = (0, jnp.where(odd == 1, sub, before), 1 - odd)
    send_row = (1, above, 1)
    keep_col = (0, jnp.where(odd == 1, before, sub), odd)
    keep_row = (1, sub, 0)
    return send_col, send_row, keep_col, keep_row


def apply_kernel(
    nk, cols, index_hbm, owner_hbm, margin_hbm, stiff_hbm, modes_hbm,
    applied_ref, send_col_ref, send_row_ref,
    index, owners, lists, stiff, modes, total, small_sem, mode_sem, stiff_sem,
):
    small = [
        pltpu.make_async_copy(src, dst, small_sem.at[i])
        for i, (src, dst) in enumerate(((index_hbm, index), (owner_hbm, owners), (margin_hbm, lists)))
    ]
    mode_copy = pltpu.make_async_copy(modes_hbm, modes, mode_sem)
    stiff_copies = [
        pltpu.make_async_copy(stiff_hbm.at[k], stiff.at[k], stiff_sem.at[k]) for k in range(nk)
    ]
    small[0].start()
    mode_copy.start()
    for k in range(nk):
        stiff_copies[k].start()
    small[1].start()
    small[2].start()
    total[...] = jnp.zeros_like(total)
    small[0].wait()
    mode_copy.wait()
    for k in range(nk):
        stiff_copies[k].wait()
        product = jnp.dot(stiff[k], modes[index[1, k]], preferred_element_type=F32)
        a = index[0, k]
        total[a] = total[a] + product
    for a in range(applied_ref.shape[0]):
        applied_ref[a] = total[a].astype(BF16)
    small[1].wait()
    small[2].wait()
    _, _, sub, odd = place()
    send_col, send_row, _, _ = sides(sub, odd, cols)
    for out, (direction, first, side) in ((send_col_ref, send_col), (send_row_ref, send_row)):
        for j in range(out.shape[0]):
            block, use_applied = side_block(owners, lists, direction, first, side, j)

            @pl.when(use_applied)
            def _():
                out[j] = applied_ref[block]

            @pl.when(jnp.logical_not(use_applied))
            def _():
                out[j] = modes[block]


def middle_kernel(
    cols, owners, lists, modes, applied, stored, diag_ref, keep_col_ref, keep_row_ref,
    zeros, total, zero_sem,
):
    zeros[...] = jnp.zeros_like(zeros)
    fills = [
        pltpu.make_async_copy(zeros, stored.at[i], zero_sem.at[i]) for i in range(stored.shape[0])
    ]
    for fill in fills:
        fill.start()
    _, _, sub, odd = place()
    _, _, keep_col, keep_row = sides(sub, odd, cols)
    bs = modes.shape[1]
    for out, (direction, first, side) in ((keep_col_ref, keep_col), (keep_row_ref, keep_row)):
        for j in range(out.shape[1] // bs):
            block, use_applied = side_block(owners, lists, direction, first, side, j)

            @pl.when(use_applied)
            def _():
                out[:, j * bs : (j + 1) * bs] = applied[block].T

            @pl.when(jnp.logical_not(use_applied))
            def _():
                out[:, j * bs : (j + 1) * bs] = modes[block].T

    total[...] = jnp.zeros_like(total)

    def step(a, carry):
        total[...] += lax.dot_general(
            modes[a], applied[a], (((0,), (0,)), ((), ())), preferred_element_type=F32
        )
        return carry

    lax.fori_loop(0, modes.shape[0], step, 0)
    diag_ref[...] = total[...].astype(BF16)
    for fill in fills:
        fill.wait()


def project_kernel(diag, keep_col, keep_row, got_col, got_row, pieces):
    part = pieces.shape[1] // 3
    row_block = jnp.dot(keep_row[...], got_row[...], preferred_element_type=F32).astype(BF16)
    col_block = jnp.dot(keep_col[...], got_col[...], preferred_element_type=F32)
    odd = lax.rem(lax.axis_index("row"), 2)
    for c in range(pieces.shape[0]):
        pieces[c, 0:part] = diag[c * part : (c + 1) * part]
        pieces[c, 2 * part : 3 * part] = row_block[c * part : (c + 1) * part]

    def spread(block):
        for c in range(pieces.shape[0]):
            pieces[c, part : 2 * part] = block[c * part : (c + 1) * part]

    @pl.when(odd == 0)
    def _():
        spread(col_block.astype(BF16))

    @pl.when(odd == 1)
    def _():
        spread(col_block.T.astype(BF16))


def store_kernel(rows, received, zeroed, stored, sems):
    del zeroed
    cols = received.shape[0]
    part = received.shape[1] // 3
    row = lax.axis_index("row")
    odd = lax.rem(row, 2)
    base = row * cols

    def copies(act):
        for c in range(cols):
            act(pltpu.make_async_copy(received.at[c, 0:part], stored.at[c, base + c], sems.at[0, c]))

            def col_copy(local):
                act(
                    pltpu.make_async_copy(
                        received.at[c, part : 2 * part], stored.at[local, base + local + 1], sems.at[1, c]
                    )
                )

            if c < cols - 1:
                pl.when(odd == 0)(functools.partial(col_copy, c))
            if c > 0:
                pl.when(odd == 1)(functools.partial(col_copy, c - 1))

        @pl.when(row < rows - 1)
        def _():
            for c in range(cols):
                act(
                    pltpu.make_async_copy(
                        received.at[c, 2 * part : 3 * part], stored.at[c, base + cols + c], sems.at[2, c]
                    )
                )

    copies(lambda copy: copy.start())
    copies(lambda copy: copy.wait())


def params(mib):
    return pltpu.CompilerParams(vmem_limit_bytes=mib << 20)


def on_device(stiffness, stiffness_index, mode_basis, pair_owner, margin):
    rows = lax.axis_size("row")
    cols = lax.axis_size("col")
    nk, bs, _ = stiffness.shape
    m = mode_basis.shape[1]
    nb = mode_basis.shape[0] // bs
    ovb = margin.shape[2]
    modes = mode_basis.reshape(nb, bs, m)
    index = stiffness_index.T
    owners = pair_owner.T
    lists = margin.transpose(1, 2, 3, 0)
    shape = jax.ShapeDtypeStruct
    applied, send_col, send_row = pl.pallas_call(
        functools.partial(apply_kernel, nk, cols),
        out_shape=(shape((nb, bs, m), BF16), shape((ovb, bs, m), BF16), shape((ovb, bs, m), BF16)),
        in_specs=[ANY] * 5,
        out_specs=(VMEM, VMEM, VMEM),
        scratch_shapes=[
            pltpu.SMEM(index.shape, jnp.int32),
            pltpu.SMEM(owners.shape, jnp.int32),
            pltpu.SMEM(lists.shape, jnp.int32),
            pltpu.VMEM((nk, bs, bs), BF16),
            pltpu.VMEM((nb, bs, m), BF16),
            pltpu.VMEM((nb, bs, m), F32),
            pltpu.SemaphoreType.DMA((3,)),
            pltpu.SemaphoreType.DMA,
            pltpu.SemaphoreType.DMA((nk,)),
        ],
        compiler_params=params(20),
        cost_estimate=pl.CostEstimate(
            flops=2 * nk * bs * bs * m, bytes_accessed=2 * (stiffness.size + 2 * mode_basis.size), transcendentals=0
        ),
        name="apply",
    )(index, owners, lists, stiffness, modes)

    flat = rows * cols
    line = [(d, d - 1) for d in range(flat) if (d // cols) % 2 == 0 and d % cols > 0]
    line += [(d, d + 1) for d in range(flat) if (d // cols) % 2 == 1 and d % cols < cols - 1]
    got_col = lax.ppermute(send_col, ("row", "col"), line)
    got_row = lax.ppermute(send_row, "row", [(r, r - 1) for r in range(1, rows)])

    total = rows * cols
    part = m // cols
    stored, diag, keep_col, keep_row = pl.pallas_call(
        functools.partial(middle_kernel, cols),
        out_shape=(
            shape((cols, total, part, m), BF16),
            shape((m, m), BF16),
            shape((m, ovb * bs), BF16),
            shape((m, ovb * bs), BF16),
        ),
        in_specs=[SMEM, SMEM, VMEM, VMEM],
        out_specs=(ANY, VMEM, VMEM, VMEM),
        scratch_shapes=[
            pltpu.VMEM((total, part, m), BF16),
            pltpu.VMEM((m, m), F32),
            pltpu.SemaphoreType.DMA((cols,)),
        ],
        compiler_params=params(12),
        cost_estimate=pl.CostEstimate(
            flops=2 * mode_basis.size * m, bytes_accessed=2 * cols * total * part * m, transcendentals=0
        ),
        name="middle",
    )(owners, lists, modes, applied)

    pieces = pl.pallas_call(
        project_kernel,
        out_shape=shape((cols, 3 * part, m), BF16),
        in_specs=[VMEM] * 5,
        out_specs=VMEM,
        compiler_params=params(12),
        cost_estimate=pl.CostEstimate(
            flops=4 * ovb * bs * m * m, bytes_accessed=8 * ovb * bs * m, transcendentals=0
        ),
        name="project",
    )(diag, keep_col, keep_row, got_col.reshape(ovb * bs, m), got_row.reshape(ovb * bs, m))

    received = lax.all_to_all(pieces, "col", split_axis=0, concat_axis=0, tiled=True)

    return pl.pallas_call(
        functools.partial(store_kernel, rows),
        out_shape=shape(stored.shape, BF16),
        in_specs=[VMEM, ANY],
        out_specs=ANY,
        scratch_shapes=[pltpu.SemaphoreType.DMA((3, cols))],
        input_output_aliases={1: 0},
        compiler_params=params(12),
        name="store",
    )(received, stored)


def solution(mesh):
    return jax.shard_map(
        on_device,
        mesh=mesh,
        in_specs=(
            P(("row", "col"), None, None),
            P(("row", "col"), None),
            P(("row", "col"), None),
            P(),
            P(),
        ),
        out_specs=P("row", None, "col", None),
        check_vma=False,
    )
```

time: 167 us -> 51.1 us (0.31)
  the two profiles are of different devices: /device:TPU:2 before, /device:TPU:1 now
where the time goes in v1:
time: 51.1 us; the launch traced here: 50.7 us
  Pallas kernels  20.4 us (40%)
  blocking collectives  16.4 us (32%)
  starting transfers between devices  6.31 us (12%)
  local copies, waits for them, and re-layouts  5.68 us (11%)
  waiting for transfers between devices  1.85 us (4%)
    all_to_all x1, blocking collectives, on_device(): lax.all_to_all(pieces, 'col', split_axis=0, concat_axis=0, tiled=True)  16.4 us
    pallas_call x1, Pallas kernels, on_device(): pl.pallas_call(functools.partial(apply_kernel, nk, cols), out_shape=(shap...  12 us
    pallas_call x1, Pallas kernels, on_device(): pl.pallas_call(functools.partial(middle_kernel, cols), out_shape=(shape((...  6.71 us
    unnamed x10, local copies, waits for them, and re-layouts  5.68 us
    ppermute x1, starting transfers between devices, on_device(): got_col = lax.ppermute(send_col, ('row', 'col'), line)  4.39 us
    ppermute x1, starting transfers between devices, on_device(): lax.ppermute(send_row, 'row', [(r, r - 1) for r in range(1, rows)])  1.92 us
    ppermute x1, waiting for transfers between devices, on_device(): lax.ppermute(send_row, 'row', [(r, r - 1) for r in range(1, rows)])  1.85 us
    pallas_call x1, Pallas kernels, on_device(): pl.pallas_call(functools.partial(store_kernel, rows), out_shape=shape(sto...  1.2 us
  transfers between devices with their start and end apart: 2, of which 1 were waited for; matrix products, arithmetic and copies ran while one was open for 0% of the time, Pallas kernels for 13%

profile of v1, /device:TPU:1, one launch (start us, length us, event | category | flops | bytes accessed | tf_op | source)
XLA Modules:
  0.0 50.7 jit_solution(16914805504487290825)
XLA Ops:
  0.0 0.0 copy-start
  0.0 1.6 %copy-done = bf16[4096,256]{1,0:T(8,128)(2,1)S(1)} copy-done((bf16[4096,256]{1,0:T(8,128)(2,1)S(1)}, bf16[4096,256]{1,0:T(8,128)(2,1)}, u32[]{:S(2)}) %copy-start) | copy-done | bytes 2097176
  1.6 0.0 copy-start.1
  1.6 2.0 %copy-done.1 = bf16[28,256,256]{2,1,0:T(8,128)(2,1)S(1)} copy-done((bf16[28,256,256]{2,1,0:T(8,128)(2,1)S(1)}, bf16[28,256,256]{2,1,0:T(8,128)(2,1)}, u32[]{:S(2)}) %copy-start.1) | copy-done | bytes 3670040
  3.6 0.0 copy-start.2
  3.6 0.7 %copy-done.2 = s32[128,2,4,2]{0,3,2,1:T(2,128)S(1)} copy-done((s32[128,2,4,2]{0,3,2,1:T(2,128)S(1)}, s32[128,2,4,2]{0,3,2,1:T(2,128)}, u32[]{:S(2)}) %copy-start.2) | copy-done | bytes 8216
  4.3 0.0 copy-start.3
  4.3 0.7 %copy-done.3 = s32[128,2]{0,1:T(2,128)S(1)} copy-done((s32[128,2]{0,1:T(2,128)S(1)}, s32[128,2]{0,1:T(2,128)}, u32[]{:S(2)}) %copy-start.3) | copy-done | bytes 1048
  5.0 0.0 copy-start.4
  5.0 0.7 %copy-done.4 = s32[28,2]{0,1:T(2,128)S(1)} copy-done((s32[28,2]{0,1:T(2,128)S(1)}, s32[28,2]{0,1:T(2,128)}, u32[]{:S(2)}) %copy-start.4) | copy-done | bytes 248
  5.7 12.0 %apply.1 = (bf16[16,256,256]{2,1,0:T(8,128)(2,1)S(1)}, bf16[4,256,256]{2,1,0:T(8,128)(2,1)S(1)}, bf16[4,256,256]{2,1,0:T(8,128)(2,1)S(1)}) custom-call(s32[2,28]{1,0:T(2,128)S(1)} %bitcast.14, s32[2,128]{1,0:T(2,128)S(1)} %bitcast.12, s32[2,4,2,128]{3,2,1,0:T(2,128)S(1)} %bitcast.10, bf16[28,256,256]{2,1,0:T(8,128)(2,1)S(1)} %copy-done.1, ...), custom_call_target="tpu_custom_call" | custom-call | flops 939524096 | bytes 7864320 | tf_op jit(solution)/shard_map/apply/pallas_call | solution.py:199
  17.7 4.4 %collective-permute-start = (bf16[4,256,256]{2,1,0:T(8,128)(2,1)S(1)}, bf16[4,256,256]{2,1,0:T(8,128)(2,1)S(1)}, u32[]{:S(2)}, u32[]{:S(2)}) collective-permute-start(bf16[4,256,256]{2,1,0:T(8,128)(2,1)S(1)} %get-tuple-element.16), channel_id=1, source_target_pairs={{1,0},{2,1},{3,2},{4,3},{5,4},{6,5},{7,6},{8,7},{9,8},{10,9},{11,1... | collective-permute-start | bytes 1572872 | tf_op jit(solution)/shard_map/ppermute | solution.py:225
  22.1 1.9 %collective-permute-start.1 = (bf16[4,256,256]{2,1,0:T(8,128)(2,1)S(1)}, bf16[4,256,256]{2,1,0:T(8,128)(2,1)S(1)}, u32[]{:S(2)}, u32[]{:S(2)}) collective-permute-start(bf16[4,256,256]{2,1,0:T(8,128)(2,1)S(1)} %get-tuple-element.17), channel_id=1, source_target_pairs={{16,0},{32,16},{48,32},{64,48},{80,64},{96,80},{112,96},{17,1},{33... | collective-permute-start | bytes 1572872 | tf_op jit(solution)/shard_map/ppermute | solution.py:226
  24.0 6.7 %middle.1 = (bf16[16,128,16,256]{3,2,1,0:T(8,128)(2,1)}, bf16[256,256]{1,0:T(8,128)(2,1)S(1)}, bf16[256,1024]{1,0:T(8,128)(2,1)S(1)}, bf16[256,1024]{1,0:T(8,128)(2,1)S(1)}) custom-call(s32[2,128]{1,0:T(2,128)S(1)} %bitcast.13, s32[2,4,2,128]{3,2,1,0:T(2,128)S(1)} %bitcast.11, bf16[16,256,256]{2,1,0:T(8,128)(2,1)S(1)} %bitcast.7, ...), custom_call_target="tpu_custom_call" | custom-call | flops 536870912 | bytes 16777216 | tf_op jit(solution)/shard_map/middle/pallas_call | solution.py:230
  30.7 0.0 collective-permute-done
  30.7 1.8 %collective-permute-done.1 = bf16[4,256,256]{2,1,0:T(8,128)(2,1)S(1)} collective-permute-done((bf16[4,256,256]{2,1,0:T(8,128)(2,1)S(1)}, bf16[4,256,256]{2,1,0:T(8,128)(2,1)S(1)}, u32[]{:S(2)}, u32[]{:S(2)}) %collective-permute-start.1) | collective-permute-done | bytes 524320 | tf_op jit(solution)/shard_map/ppermute | solution.py:226
  32.6 0.5 %project.1 = bf16[16,48,256]{2,1,0:T(8,128)(2,1)S(1)} custom-call(bf16[256,256]{1,0:T(8,128)(2,1)S(1)} %get-tuple-element.13.diag, bf16[256,1024]{1,0:T(8,128)(2,1)S(1)} %get-tuple-element.14.keep_col, bf16[256,1024]{1,0:T(8,128)(2,1)S(1)} %get-tuple-element.15.keep_row, bf16[1024,256]{1,0:T(8,128)(2,1)S(1)} %bitcast.8, bf16[1024,256]{1,0:T(8,128)(2,1)S(1)} %bitcast.9), custom_call_target="tpu_custom_call" | custom-call | flops 268435456 | bytes 2097152 | tf_op jit(solution)/shard_map/project/pallas_call | solution.py:252
  33.1 16.4 %all_to_all.5.received = bf16[16,48,256]{2,1,0:T(8,128)(2,1)S(1)} all-to-all(bf16[16,48,256]{2,1,0:T(8,128)(2,1)S(1)} %project.1), channel_id=1, replica_groups=mesh['row'=8,'col'=16] {'col'}, dimensions={0} | all-to-all | bytes 786432 | tf_op jit(solution)/shard_map/all_to_all | solution.py:264
  49.5 1.2 %store.1 = bf16[16,128,16,256]{3,2,1,0:T(8,128)(2,1)} custom-call(bf16[16,48,256]{2,1,0:T(8,128)(2,1)S(1)} %all_to_all.5.received, bf16[16,128,16,256]{3,2,1,0:T(8,128)(2,1)} %get-tuple-element.18.zeroed), custom_call_target="tpu_custom_call", output_to_operand_aliasing={{}: (1, {})} | custom-call | tf_op jit(solution)/shard_map/store/pallas_call | solution.py:266
Async XLA Ops:
  0.0 1.6 %copy-start = (bf16[4096,256]{1,0:T(8,128)(2,1)S(1)}, bf16[4096,256]{1,0:T(8,128)(2,1)}, u32[]{:S(2)}) copy-start(bf16[4096,256]{1,0:T(8,128)(2,1)} %param.7) | copy-start | bytes 6291460
  1.6 2.0 %copy-start.1 = (bf16[28,256,256]{2,1,0:T(8,128)(2,1)S(1)}, bf16[28,256,256]{2,1,0:T(8,128)(2,1)}, u32[]{:S(2)}) copy-start(bf16[28,256,256]{2,1,0:T(8,128)(2,1)} %stiff_hbm.1) | copy-start | bytes 11010052
  3.6 0.7 %copy-start.2 = (s32[128,2,4,2]{0,3,2,1:T(2,128)S(1)}, s32[128,2,4,2]{0,3,2,1:T(2,128)}, u32[]{:S(2)}) copy-start(s32[128,2,4,2]{0,3,2,1:T(2,128)} %param.9) | copy-start | bytes 24580
  4.3 0.7 %copy-start.3 = (s32[128,2]{0,1:T(2,128)S(1)}, s32[128,2]{0,1:T(2,128)}, u32[]{:S(2)}) copy-start(s32[128,2]{0,1:T(2,128)} %param.8) | copy-start | bytes 3076
  5.0 0.7 %copy-start.4 = (s32[28,2]{0,1:T(2,128)S(1)}, s32[28,2]{0,1:T(2,128)}, u32[]{:S(2)}) copy-start(s32[28,2]{0,1:T(2,128)} %param.6) | copy-start | bytes 676
  17.7 13.0 %collective-permute-start = (bf16[4,256,256]{2,1,0:T(8,128)(2,1)S(1)}, bf16[4,256,256]{2,1,0:T(8,128)(2,1)S(1)}, u32[]{:S(2)}, u32[]{:S(2)}) collective-permute-start(bf16[4,256,256]{2,1,0:T(8,128)(2,1)S(1)} %get-tuple-element.16), channel_id=1, source_target_pairs={{1,0},{2,1},{3,2},{4,3},{5,4},{6,5},{7,6},{8,7},{9,8},{10,9},{11,1... | collective-permute-start | bytes 1572872 | tf_op jit(solution)/shard_map/ppermute | solution.py:225
  22.1 10.5 %collective-permute-start.1 = (bf16[4,256,256]{2,1,0:T(8,128)(2,1)S(1)}, bf16[4,256,256]{2,1,0:T(8,128)(2,1)S(1)}, u32[]{:S(2)}, u32[]{:S(2)}) collective-permute-start(bf16[4,256,256]{2,1,0:T(8,128)(2,1)S(1)} %get-tuple-element.17), channel_id=1, source_target_pairs={{16,0},{32,16},{48,32},{64,48},{80,64},{96,80},{112,96},{17,1},{33... | collective-permute-start | bytes 1572872 | tf_op jit(solution)/shard_map/ppermute | solution.py:226

commit v2 on v1

--- a/solution.py
+++ b/solution.py
@@ -9,9 +9,8 @@
 
 F32 = jnp.float32
 BF16 = jnp.bfloat16
-ANY = pl.BlockSpec(memory_space=pl.ANY)
+HBM = pl.BlockSpec(memory_space=pltpu.HBM)
 VMEM = pl.BlockSpec(memory_space=pltpu.VMEM)
-SMEM = pl.BlockSpec(memory_space=pltpu.SMEM)
 
 
 def place():
@@ -37,45 +36,47 @@
 
 
 def apply_kernel(
-    nk, cols, index_hbm, owner_hbm, margin_hbm, stiff_hbm, modes_hbm,
-    applied_ref, send_col_ref, send_row_ref,
-    index, owners, lists, stiff, modes, total, small_sem, mode_sem, stiff_sem,
+    nk, cols, groups, index_hbm, owner_hbm, margin_hbm, stiff_hbm, modes_hbm,
+    total, modes, send_col_ref, send_row_ref,
+    index, owners, lists, stiff, small_sem, mode_sem, stiff_sem,
 ):
     small = [
         pltpu.make_async_copy(src, dst, small_sem.at[i])
         for i, (src, dst) in enumerate(((index_hbm, index), (owner_hbm, owners), (margin_hbm, lists)))
     ]
     mode_copy = pltpu.make_async_copy(modes_hbm, modes, mode_sem)
+    edges = [nk * g // groups for g in range(groups + 1)]
     stiff_copies = [
-        pltpu.make_async_copy(stiff_hbm.at[k], stiff.at[k], stiff_sem.at[k]) for k in range(nk)
+        pltpu.make_async_copy(
+            stiff_hbm.at[pl.ds(lo, hi - lo)], stiff.at[pl.ds(lo, hi - lo)], stiff_sem.at[g]
+        )
+        for g, (lo, hi) in enumerate(zip(edges, edges[1:]))
     ]
     small[0].start()
     mode_copy.start()
-    for k in range(nk):
-        stiff_copies[k].start()
+    for copy in stiff_copies:
+        copy.start()
     small[1].start()
     small[2].start()
     total[...] = jnp.zeros_like(total)
-    small[0].wait()
+    for copy in small:
+        copy.wait()
     mode_copy.wait()
-    for k in range(nk):
-        stiff_copies[k].wait()
-        product = jnp.dot(stiff[k], modes[index[1, k]], preferred_element_type=F32)
-        a = index[0, k]
-        total[a] = total[a] + product
-    for a in range(applied_ref.shape[0]):
-        applied_ref[a] = total[a].astype(BF16)
-    small[1].wait()
-    small[2].wait()
+    for g in range(groups):
+        stiff_copies[g].wait()
+        for k in range(edges[g], edges[g + 1]):
+            product = jnp.dot(stiff[k], modes[index[1, k]], preferred_element_type=F32)
+            a = index[0, k]
+            total[a] = total[a] + product
     _, _, sub, odd = place()
     send_col, send_row, _, _ = sides(sub, odd, cols)
-    for out, (direction, first, side) in ((send_col_ref, send_col), (send_row_ref, send_row)):
+    for out, (direction, first, side) in ((send_row_ref, send_row), (send_col_ref, send_col)):
         for j in range(out.shape[0]):
             block, use_applied = side_block(owners, lists, direction, first, side, j)
 
             @pl.when(use_applied)
             def _():
-                out[j] = applied_ref[block]
+                out[j] = total[block].astype(BF16)
 
             @pl.when(jnp.logical_not(use_applied))
             def _():
@@ -83,15 +84,33 @@
 
 
 def middle_kernel(
-    cols, owners, lists, modes, applied, stored, diag_ref, keep_col_ref, keep_row_ref,
-    zeros, total, zero_sem,
+    cols, owner_hbm, margin_hbm, modes, applied, stored, diag_ref, keep_col_ref, keep_row_ref,
+    owners, lists, zeros, total, small_sem, zero_sem,
 ):
+    small = [
+        pltpu.make_async_copy(src, dst, small_sem.at[i])
+        for i, (src, dst) in enumerate(((owner_hbm, owners), (margin_hbm, lists)))
+    ]
+    for copy in small:
+        copy.start()
     zeros[...] = jnp.zeros_like(zeros)
     fills = [
         pltpu.make_async_copy(zeros, stored.at[i], zero_sem.at[i]) for i in range(stored.shape[0])
     ]
     for fill in fills:
         fill.start()
+    total[...] = jnp.zeros_like(total)
+
+    def step(a, carry):
+        total[...] += lax.dot_general(
+            modes[a], applied[a].astype(BF16), (((0,), (0,)), ((), ())), preferred_element_type=F32
+        )
+        return carry
+
+    lax.fori_loop(0, modes.shape[0], step, 0)
+    diag_ref[...] = total[...].astype(BF16)
+    for copy in small:
+        copy.wait()
     _, _, sub, odd = place()
     _, _, keep_col, keep_row = sides(sub, odd, cols)
     bs = modes.shape[1]
@@ -101,22 +120,12 @@
 
             @pl.when(use_applied)
             def _():
-                out[:, j * bs : (j + 1) * bs] = applied[block].T
+                out[:, j * bs : (j + 1) * bs] = applied[block].astype(BF16).T
 
             @pl.when(jnp.logical_not(use_applied))
             def _():
                 out[:, j * bs : (j + 1) * bs] = modes[block].T
 
-    total[...] = jnp.zeros_like(total)
-
-    def step(a, carry):
-        total[...] += lax.dot_general(
-            modes[a], applied[a], (((0,), (0,)), ((), ())), preferred_element_type=F32
-        )
-        return carry
-
-    lax.fori_loop(0, modes.shape[0], step, 0)
-    diag_ref[...] = total[...].astype(BF16)
     for fill in fills:
         fill.wait()
 
@@ -195,63 +204,69 @@
     index = stiffness_index.T
     owners = pair_owner.T
     lists = margin.transpose(1, 2, 3, 0)
-    shape = jax.ShapeDtypeStruct
-    applied, send_col, send_row = pl.pallas_call(
-        functools.partial(apply_kernel, nk, cols),
-        out_shape=(shape((nb, bs, m), BF16), shape((ovb, bs, m), BF16), shape((ovb, bs, m), BF16)),
-        in_specs=[ANY] * 5,
-        out_specs=(VMEM, VMEM, VMEM),
+    groups = 2
+    hbm = lambda x: pltpu.with_memory_space_constraint(x, pltpu.HBM)
+    total, modes_near, send_col, send_row = pl.pallas_call(
+        functools.partial(apply_kernel, nk, cols, groups),
+        out_shape=(
+            pltpu.VMEM((nb, bs, m), F32),
+            pltpu.VMEM((nb, bs, m), BF16),
+            pltpu.VMEM((ovb, bs, m), BF16),
+            pltpu.VMEM((ovb, bs, m), BF16),
+        ),
+        in_specs=[HBM] * 5,
+        out_specs=(VMEM,) * 4,
         scratch_shapes=[
             pltpu.SMEM(index.shape, jnp.int32),
             pltpu.SMEM(owners.shape, jnp.int32),
             pltpu.SMEM(lists.shape, jnp.int32),
             pltpu.VMEM((nk, bs, bs), BF16),
-            pltpu.VMEM((nb, bs, m), BF16),
-            pltpu.VMEM((nb, bs, m), F32),
             pltpu.SemaphoreType.DMA((3,)),
             pltpu.SemaphoreType.DMA,
-            pltpu.SemaphoreType.DMA((nk,)),
+            pltpu.SemaphoreType.DMA((groups,)),
         ],
         compiler_params=params(20),
         cost_estimate=pl.CostEstimate(
             flops=2 * nk * bs * bs * m, bytes_accessed=2 * (stiffness.size + 2 * mode_basis.size), transcendentals=0
         ),
         name="apply",
-    )(index, owners, lists, stiffness, modes)
-
+    )(hbm(index), hbm(owners), hbm(lists), hbm(stiffness), hbm(modes))
+
+    got_row = lax.ppermute(send_row, "row", [(r, r - 1) for r in range(1, rows)])
     flat = rows * cols
     line = [(d, d - 1) for d in range(flat) if (d // cols) % 2 == 0 and d % cols > 0]
     line += [(d, d + 1) for d in range(flat) if (d // cols) % 2 == 1 and d % cols < cols - 1]
     got_col = lax.ppermute(send_col, ("row", "col"), line)
-    got_row = lax.ppermute(send_row, "row", [(r, r - 1) for r in range(1, rows)])
-
-    total = rows * cols
+
     part = m // cols
     stored, diag, keep_col, keep_row = pl.pallas_call(
         functools.partial(middle_kernel, cols),
         out_shape=(
-            shape((cols, total, part, m), BF16),
-            shape((m, m), BF16),
-            shape((m, ovb * bs), BF16),
-            shape((m, ovb * bs), BF16),
-        ),
-        in_specs=[SMEM, SMEM, VMEM, VMEM],
-        out_specs=(ANY, VMEM, VMEM, VMEM),
+            pltpu.HBM((cols, flat, part, m), BF16),
+            pltpu.VMEM((m, m), BF16),
+            pltpu.VMEM((m, ovb * bs), BF16),
+            pltpu.VMEM((m, ovb * bs), BF16),
+        ),
+        in_specs=[HBM, HBM, VMEM, VMEM],
+        out_specs=(HBM, VMEM, VMEM, VMEM),
         scratch_shapes=[
-            pltpu.VMEM((total, part, m), BF16),
+            pltpu.SMEM(owners.shape, jnp.int32),
+            pltpu.SMEM(lists.shape, jnp.int32),
+            pltpu.VMEM((flat, part, m), BF16),
             pltpu.VMEM((m, m), F32),
+            pltpu.SemaphoreType.DMA((2,)),
             pltpu.SemaphoreType.DMA((cols,)),
         ],
         compiler_params=params(12),
         cost_estimate=pl.CostEstimate(
-            flops=2 * mode_basis.size * m, bytes_accessed=2 * cols * total * part * m, transcendentals=0
+            flops=2 * mode_basis.size * m, bytes_accessed=2 * cols * flat * part * m, transcendentals=0
         ),
         name="middle",
-    )(owners, lists, modes, applied)
+    )(hbm(owners), hbm(lists), modes_near, total)
 
     pieces = pl.pallas_call(
         project_kernel,
-        out_shape=shape((cols, 3 * part, m), BF16),
+        out_shape=pltpu.VMEM((cols, 3 * part, m), BF16),
         in_specs=[VMEM] * 5,
         out_specs=VMEM,
         compiler_params=params(12),
@@ -265,9 +280,9 @@
 
     return pl.pallas_call(
         functools.partial(store_kernel, rows),
-        out_shape=shape(stored.shape, BF16),
-        in_specs=[VMEM, ANY],
-        out_specs=ANY,
+        out_shape=pltpu.HBM(stored.shape, BF16),
+        in_specs=[VMEM, HBM],
+        out_specs=HBM,
         scratch_shapes=[pltpu.SemaphoreType.DMA((3, cols))],
         input_output_aliases={1: 0},
         compiler_params=params(12),

time: 51.1 us -> 37.1 us (0.73)
  Pallas kernels: 20.4 us -> 11.5 us
  local copies, waits for them, and re-layouts: 5.68 us -> 0 us
  waiting for transfers between devices: 1.85 us -> 2.51 us
    pallas_call x4, Pallas kernels: 20.4 us -> 11.5 us  [the longest x1 6.05 us: on_device(): pl.pallas_call(functools.partial(middle_kernel, cols), out_shape=(pltpu.H...]
    unnamed x10 -> x0, local copies, waits for them, and re-layouts: 5.68 us -> none
    ppermute x1, waiting for transfers between devices: 1.85 us -> 2.51 us  [on_device(): lax.ppermute(send_row, 'row', [(r, r - 1) for r in range(1, rows)])]
  transfers between devices with their start and end apart: 2 -> 2, of which waited for: 1 -> 1; matrix products, arithmetic and copies ran while one was open for 0% -> 0% of each run, Pallas kernels for 13% -> 16%
where the time goes in v2:
time: 37.1 us; the launch traced here: 36.8 us
  blocking collectives  16.4 us (44%)
  Pallas kernels  11.5 us (31%)
  starting transfers between devices  6.34 us (17%)
  waiting for transfers between devices  2.51 us (7%)
    all_to_all x1, blocking collectives, on_device(): lax.all_to_all(pieces, 'col', split_axis=0, concat_axis=0, tiled=True)  16.4 us
    pallas_call x1, Pallas kernels, on_device(): pl.pallas_call(functools.partial(middle_kernel, cols), out_shape=(pltpu.H...  6.05 us
    ppermute x1, starting transfers between devices, on_device(): got_col = lax.ppermute(send_col, ('row', 'col'), line)  4.42 us
    pallas_call x1, Pallas kernels, on_device(): pl.pallas_call(functools.partial(apply_kernel, nk, cols, groups), out_sha...  3.76 us
    ppermute x1, waiting for transfers between devices, on_device(): lax.ppermute(send_row, 'row', [(r, r - 1) for r in range(1, rows)])  2.51 us
    ppermute x1, starting transfers between devices, on_device(): lax.ppermute(send_row, 'row', [(r, r - 1) for r in range(1, rows)])  1.92 us
    pallas_call x1, Pallas kernels, on_device(): pl.pallas_call(functools.partial(store_kernel, rows), out_shape=pltpu.HBM...  1.2 us
  transfers between devices with their start and end apart: 2, of which 1 were waited for; matrix products, arithmetic and copies ran while one was open for 0% of the time, Pallas kernels for 16%

profile of v2, /device:TPU:1, one launch (start us, length us, event | category | flops | bytes accessed | tf_op | source)
XLA Modules:
  0.0 36.8 jit_solution(2288264067944381986)
XLA Ops:
  0.0 3.8 %apply.1 = (f32[16,256,256]{2,1,0:T(8,128)S(1)}, bf16[16,256,256]{2,1,0:T(8,128)(2,1)S(1)}, bf16[4,256,256]{2,1,0:T(8,128)(2,1)S(1)}, bf16[4,256,256]{2,1,0:T(8,128)(2,1)S(1)}) custom-call(s32[2,28]{1,0:T(2,128)} %bitcast.13, s32[2,128]{1,0:T(2,128)} %bitcast.11, s32[2,4,2,128]{3,2,1,0:T(2,128)} %bitcast.9, bf16[28,256,256]{2,1,0:T(8,128)(2,1)} %stiff_hbm.1, ...), custom_call_target="tpu_custom_call" | custom-call | flops 939524096 | bytes 7864320 | tf_op jit(solution)/shard_map/apply/pallas_call | solution.py:209
  3.8 4.4 %collective-permute-start = (bf16[4,256,256]{2,1,0:T(8,128)(2,1)S(1)}, bf16[4,256,256]{2,1,0:T(8,128)(2,1)S(1)}, u32[]{:S(2)}, u32[]{:S(2)}) collective-permute-start(bf16[4,256,256]{2,1,0:T(8,128)(2,1)S(1)} %get-tuple-element.18), channel_id=1, source_target_pairs={{1,0},{2,1},{3,2},{4,3},{5,4},{6,5},{7,6},{8,7},{9,8},{10,9},{11,1... | collective-permute-start | bytes 1572872 | tf_op jit(solution)/shard_map/ppermute | solution.py:239
  8.2 1.9 %collective-permute-start.1 = (bf16[4,256,256]{2,1,0:T(8,128)(2,1)S(1)}, bf16[4,256,256]{2,1,0:T(8,128)(2,1)S(1)}, u32[]{:S(2)}, u32[]{:S(2)}) collective-permute-start(bf16[4,256,256]{2,1,0:T(8,128)(2,1)S(1)} %get-tuple-element.19), channel_id=1, source_target_pairs={{16,0},{32,16},{48,32},{64,48},{80,64},{96,80},{112,96},{17,1},{33... | collective-permute-start | bytes 1572872 | tf_op jit(solution)/shard_map/ppermute | solution.py:235
  10.1 6.0 %middle.1 = (bf16[16,128,16,256]{3,2,1,0:T(8,128)(2,1)}, bf16[256,256]{1,0:T(8,128)(2,1)S(1)}, bf16[256,1024]{1,0:T(8,128)(2,1)S(1)}, bf16[256,1024]{1,0:T(8,128)(2,1)S(1)}) custom-call(s32[2,128]{1,0:T(2,128)} %bitcast.12, s32[2,4,2,128]{3,2,1,0:T(2,128)} %bitcast.10, bf16[16,256,256]{2,1,0:T(8,128)(2,1)S(1)} %get-tuple-element.13.modes, ...), custom_call_target="tpu_custom_call" | custom-call | flops 536870912 | bytes 16777216 | tf_op jit(solution)/shard_map/middle/pallas_call | solution.py:242
  16.2 0.0 collective-permute-done
  16.2 2.5 %collective-permute-done.1 = bf16[4,256,256]{2,1,0:T(8,128)(2,1)S(1)} collective-permute-done((bf16[4,256,256]{2,1,0:T(8,128)(2,1)S(1)}, bf16[4,256,256]{2,1,0:T(8,128)(2,1)S(1)}, u32[]{:S(2)}, u32[]{:S(2)}) %collective-permute-start.1) | collective-permute-done | bytes 524320 | tf_op jit(solution)/shard_map/ppermute | solution.py:235
  18.7 0.5 %project.1 = bf16[16,48,256]{2,1,0:T(8,128)(2,1)S(1)} custom-call(bf16[256,256]{1,0:T(8,128)(2,1)S(1)} %get-tuple-element.15.diag, bf16[256,1024]{1,0:T(8,128)(2,1)S(1)} %get-tuple-element.16.keep_col, bf16[256,1024]{1,0:T(8,128)(2,1)S(1)} %get-tuple-element.17.keep_row, bf16[1024,256]{1,0:T(8,128)(2,1)S(1)} %bitcast.6, bf16[1024,256]{1,0:T(8,128)(2,1)S(1)} %bitcast.7), custom_call_target="tpu_custom_call" | custom-call | flops 268435456 | bytes 2097152 | tf_op jit(solution)/shard_map/project/pallas_call | solution.py:267
  19.2 16.4 %all_to_all.5.received = bf16[16,48,256]{2,1,0:T(8,128)(2,1)S(1)} all-to-all(bf16[16,48,256]{2,1,0:T(8,128)(2,1)S(1)} %project.1), channel_id=1, replica_groups=mesh['row'=8,'col'=16] {'col'}, dimensions={0} | all-to-all | bytes 786432 | tf_op jit(solution)/shard_map/all_to_all | solution.py:279
  35.6 1.2 %store.1 = bf16[16,128,16,256]{3,2,1,0:T(8,128)(2,1)} custom-call(bf16[16,48,256]{2,1,0:T(8,128)(2,1)S(1)} %all_to_all.5.received, bf16[16,128,16,256]{3,2,1,0:T(8,128)(2,1)} %get-tuple-element.20.zeroed), custom_call_target="tpu_custom_call", output_to_operand_aliasing={{}: (1, {})} | custom-call | tf_op jit(solution)/shard_map/store/pallas_call | solution.py:281
Async XLA Ops:
  3.8 12.4 %collective-permute-start = (bf16[4,256,256]{2,1,0:T(8,128)(2,1)S(1)}, bf16[4,256,256]{2,1,0:T(8,128)(2,1)S(1)}, u32[]{:S(2)}, u32[]{:S(2)}) collective-permute-start(bf16[4,256,256]{2,1,0:T(8,128)(2,1)S(1)} %get-tuple-element.18), channel_id=1, source_target_pairs={{1,0},{2,1},{3,2},{4,3},{5,4},{6,5},{7,6},{8,7},{9,8},{10,9},{11,1... | collective-permute-start | bytes 1572872 | tf_op jit(solution)/shard_map/ppermute | solution.py:239
  8.2 10.5 %collective-permute-start.1 = (bf16[4,256,256]{2,1,0:T(8,128)(2,1)S(1)}, bf16[4,256,256]{2,1,0:T(8,128)(2,1)S(1)}, u32[]{:S(2)}, u32[]{:S(2)}) collective-permute-start(bf16[4,256,256]{2,1,0:T(8,128)(2,1)S(1)} %get-tuple-element.19), channel_id=1, source_target_pairs={{16,0},{32,16},{48,32},{64,48},{80,64},{96,80},{112,96},{17,1},{33... | collective-permute-start | bytes 1572872 | tf_op jit(solution)/shard_map/ppermute | solution.py:235

commit v3 on v2

--- a/solution.py
+++ b/solution.py
@@ -18,6 +18,12 @@
     col = lax.axis_index("col")
     sub = row * lax.axis_size("col") + col
     return row, col, sub, lax.rem(row, 2)
+
+
+def exchange_order(cols):
+    side = int(cols**0.5)
+    y0, z0 = side // 2, side // 2
+    return [(y0 + i + j) % side * side + (z0 + j) % side for i in range(side) for j in range(side)]
 
 
 def side_block(owners, lists, direction, first, side, j):
@@ -130,18 +136,18 @@
         fill.wait()
 
 
-def project_kernel(diag, keep_col, keep_row, got_col, got_row, pieces):
+def project_kernel(order, diag, keep_col, keep_row, got_col, got_row, pieces):
     part = pieces.shape[1] // 3
     row_block = jnp.dot(keep_row[...], got_row[...], preferred_element_type=F32).astype(BF16)
     col_block = jnp.dot(keep_col[...], got_col[...], preferred_element_type=F32)
     odd = lax.rem(lax.axis_index("row"), 2)
-    for c in range(pieces.shape[0]):
-        pieces[c, 0:part] = diag[c * part : (c + 1) * part]
-        pieces[c, 2 * part : 3 * part] = row_block[c * part : (c + 1) * part]
+    for p, c in enumerate(order):
+        pieces[p, 0:part] = diag[c * part : (c + 1) * part]
+        pieces[p, 2 * part : 3 * part] = row_block[c * part : (c + 1) * part]
 
     def spread(block):
-        for c in range(pieces.shape[0]):
-            pieces[c, part : 2 * part] = block[c * part : (c + 1) * part]
+        for p, c in enumerate(order):
+            pieces[p, part : 2 * part] = block[c * part : (c + 1) * part]
 
     @pl.when(odd == 0)
     def _():
@@ -152,7 +158,7 @@
         spread(col_block.T.astype(BF16))
 
 
-def store_kernel(rows, received, zeroed, stored, sems):
+def store_kernel(rows, order, received, zeroed, stored, sems):
     del zeroed
     cols = received.shape[0]
     part = received.shape[1] // 3
@@ -161,27 +167,27 @@
     base = row * cols
 
     def copies(act):
-        for c in range(cols):
-            act(pltpu.make_async_copy(received.at[c, 0:part], stored.at[c, base + c], sems.at[0, c]))
-
-            def col_copy(local):
+        for p, c in enumerate(order):
+            act(pltpu.make_async_copy(received.at[p, 0:part], stored.at[c, base + c], sems.at[0, c]))
+
+            def col_copy(p, local):
                 act(
                     pltpu.make_async_copy(
-                        received.at[c, part : 2 * part], stored.at[local, base + local + 1], sems.at[1, c]
+                        received.at[p, part : 2 * part], stored.at[local, base + local + 1], sems.at[1, p]
                     )
                 )
 
             if c < cols - 1:
-                pl.when(odd == 0)(functools.partial(col_copy, c))
+                pl.when(odd == 0)(functools.partial(col_copy, p, c))
             if c > 0:
-                pl.when(odd == 1)(functools.partial(col_copy, c - 1))
+                pl.when(odd == 1)(functools.partial(col_copy, p, c - 1))
 
         @pl.when(row < rows - 1)
         def _():
-            for c in range(cols):
+            for p, c in enumerate(order):
                 act(
                     pltpu.make_async_copy(
-                        received.at[c, 2 * part : 3 * part], stored.at[c, base + cols + c], sems.at[2, c]
+                        received.at[p, 2 * part : 3 * part], stored.at[c, base + cols + c], sems.at[2, c]
                     )
                 )
 
@@ -264,8 +270,9 @@
         name="middle",
     )(hbm(owners), hbm(lists), modes_near, total)
 
+    order = exchange_order(cols)
     pieces = pl.pallas_call(
-        project_kernel,
+        functools.partial(project_kernel, order),
         out_shape=pltpu.VMEM((cols, 3 * part, m), BF16),
         in_specs=[VMEM] * 5,
         out_specs=VMEM,
@@ -276,10 +283,12 @@
         name="project",
     )(diag, keep_col, keep_row, got_col.reshape(ovb * bs, m), got_row.reshape(ovb * bs, m))
 
-    received = lax.all_to_all(pieces, "col", split_axis=0, concat_axis=0, tiled=True)
+    received = lax.all_to_all(
+        pieces, "col", split_axis=0, concat_axis=0, axis_index_groups=[order], tiled=True
+    )
 
     return pl.pallas_call(
-        functools.partial(store_kernel, rows),
+        functools.partial(store_kernel, rows, order),
         out_shape=pltpu.HBM(stored.shape, BF16),
         in_specs=[VMEM, HBM],
         out_specs=HBM,

time: 37.1 us -> 35.3 us (0.951)
  blocking collectives: 16.4 us -> 14.7 us
    all_to_all x1, blocking collectives: 16.4 us -> 14.7 us  [on_device(): lax.all_to_all(pieces, 'col', split_axis=0, concat_axis=0, axis_index_gro...]
  transfers between devices with their start and end apart: 2 -> 2, of which waited for: 1 -> 1; matrix products, arithmetic and copies ran while one was open for 0% -> 0% of each run, Pallas kernels for 16% -> 17%
where the time goes in v3:
time: 35.3 us; the launch traced here: 35.1 us
  blocking collectives  14.7 us (42%)
  Pallas kernels  11.5 us (33%)
  starting transfers between devices  6.32 us (18%)
  waiting for transfers between devices  2.51 us (7%)
    all_to_all x1, blocking collectives, on_device(): lax.all_to_all(pieces, 'col', split_axis=0, concat_axis=0, axis_index_gro...  14.7 us
    pallas_call x1, Pallas kernels, on_device(): pl.pallas_call(functools.partial(middle_kernel, cols), out_shape=(pltpu.H...  6.05 us
    ppermute x1, starting transfers between devices, on_device(): got_col = lax.ppermute(send_col, ('row', 'col'), line)  4.4 us
    pallas_call x1, Pallas kernels, on_device(): pl.pallas_call(functools.partial(apply_kernel, nk, cols, groups), out_sha...  3.76 us
    ppermute x1, waiting for transfers between devices, on_device(): lax.ppermute(send_row, 'row', [(r, r - 1) for r in range(1, rows)])  2.51 us
    ppermute x1, starting transfers between devices, on_device(): lax.ppermute(send_row, 'row', [(r, r - 1) for r in range(1, rows)])  1.92 us
    pallas_call x1, Pallas kernels, on_device(): pl.pallas_call(functools.partial(store_kernel, rows, order), out_shape=pl...  1.2 us
  transfers between devices with their start and end apart: 2, of which 1 were waited for; matrix products, arithmetic and copies ran while one was open for 0% of the time, Pallas kernels for 17%

profile of v3, /device:TPU:1, one launch (start us, length us, event | category | flops | bytes accessed | tf_op | source)
XLA Modules:
  0.0 35.1 jit_solution(1096612405890015797)
XLA Ops:
  0.0 3.8 %apply.1 = (f32[16,256,256]{2,1,0:T(8,128)S(1)}, bf16[16,256,256]{2,1,0:T(8,128)(2,1)S(1)}, bf16[4,256,256]{2,1,0:T(8,128)(2,1)S(1)}, bf16[4,256,256]{2,1,0:T(8,128)(2,1)S(1)}) custom-call(s32[2,28]{1,0:T(2,128)} %bitcast.13, s32[2,128]{1,0:T(2,128)} %bitcast.11, s32[2,4,2,128]{3,2,1,0:T(2,128)} %bitcast.9, bf16[28,256,256]{2,1,0:T(8,128)(2,1)} %stiff_hbm.1, ...), custom_call_target="tpu_custom_call" | custom-call | flops 939524096 | bytes 7864320 | tf_op jit(solution)/shard_map/apply/pallas_call | solution.py:215
  3.8 4.4 %collective-permute-start = (bf16[4,256,256]{2,1,0:T(8,128)(2,1)S(1)}, bf16[4,256,256]{2,1,0:T(8,128)(2,1)S(1)}, u32[]{:S(2)}, u32[]{:S(2)}) collective-permute-start(bf16[4,256,256]{2,1,0:T(8,128)(2,1)S(1)} %get-tuple-element.18), channel_id=1, source_target_pairs={{1,0},{2,1},{3,2},{4,3},{5,4},{6,5},{7,6},{8,7},{9,8},{10,9},{11,1... | collective-permute-start | bytes 1572872 | tf_op jit(solution)/shard_map/ppermute | solution.py:245
  8.2 1.9 %collective-permute-start.1 = (bf16[4,256,256]{2,1,0:T(8,128)(2,1)S(1)}, bf16[4,256,256]{2,1,0:T(8,128)(2,1)S(1)}, u32[]{:S(2)}, u32[]{:S(2)}) collective-permute-start(bf16[4,256,256]{2,1,0:T(8,128)(2,1)S(1)} %get-tuple-element.19), channel_id=1, source_target_pairs={{16,0},{32,16},{48,32},{64,48},{80,64},{96,80},{112,96},{17,1},{33... | collective-permute-start | bytes 1572872 | tf_op jit(solution)/shard_map/ppermute | solution.py:241
  10.1 6.0 %middle.1 = (bf16[16,128,16,256]{3,2,1,0:T(8,128)(2,1)}, bf16[256,256]{1,0:T(8,128)(2,1)S(1)}, bf16[256,1024]{1,0:T(8,128)(2,1)S(1)}, bf16[256,1024]{1,0:T(8,128)(2,1)S(1)}) custom-call(s32[2,128]{1,0:T(2,128)} %bitcast.12, s32[2,4,2,128]{3,2,1,0:T(2,128)} %bitcast.10, bf16[16,256,256]{2,1,0:T(8,128)(2,1)S(1)} %get-tuple-element.13.modes, ...), custom_call_target="tpu_custom_call" | custom-call | flops 536870912 | bytes 16777216 | tf_op jit(solution)/shard_map/middle/pallas_call | solution.py:248
  16.2 0.0 collective-permute-done
  16.2 2.5 %collective-permute-done.1 = bf16[4,256,256]{2,1,0:T(8,128)(2,1)S(1)} collective-permute-done((bf16[4,256,256]{2,1,0:T(8,128)(2,1)S(1)}, bf16[4,256,256]{2,1,0:T(8,128)(2,1)S(1)}, u32[]{:S(2)}, u32[]{:S(2)}) %collective-permute-start.1) | collective-permute-done | bytes 524320 | tf_op jit(solution)/shard_map/ppermute | solution.py:241
  18.7 0.5 %project.1 = bf16[16,48,256]{2,1,0:T(8,128)(2,1)S(1)} custom-call(bf16[256,256]{1,0:T(8,128)(2,1)S(1)} %get-tuple-element.15.diag, bf16[256,1024]{1,0:T(8,128)(2,1)S(1)} %get-tuple-element.16.keep_col, bf16[256,1024]{1,0:T(8,128)(2,1)S(1)} %get-tuple-element.17.keep_row, bf16[1024,256]{1,0:T(8,128)(2,1)S(1)} %bitcast.6, bf16[1024,256]{1,0:T(8,128)(2,1)S(1)} %bitcast.7), custom_call_target="tpu_custom_call" | custom-call | flops 268435456 | bytes 2097152 | tf_op jit(solution)/shard_map/project/pallas_call | solution.py:274
  19.2 14.7 %all_to_all.5.received = bf16[16,48,256]{2,1,0:T(8,128)(2,1)S(1)} all-to-all(bf16[16,48,256]{2,1,0:T(8,128)(2,1)S(1)} %project.1), channel_id=1, replica_groups={{10,15,0,5,14,3,4,9,2,7,8,13,6,11,12,1},{26,31,16,21,30,19,20,25,18,23,..., dimensions={0} | all-to-all | bytes 786432 | tf_op jit(solution)/shard_map/all_to_all | solution.py:286
  33.9 1.2 %store.1 = bf16[16,128,16,256]{3,2,1,0:T(8,128)(2,1)} custom-call(bf16[16,48,256]{2,1,0:T(8,128)(2,1)S(1)} %all_to_all.5.received, bf16[16,128,16,256]{3,2,1,0:T(8,128)(2,1)} %get-tuple-element.20.zeroed), custom_call_target="tpu_custom_call", output_to_operand_aliasing={{}: (1, {})} | custom-call | tf_op jit(solution)/shard_map/store/pallas_call | solution.py:290
Async XLA Ops:
  3.8 12.4 %collective-permute-start = (bf16[4,256,256]{2,1,0:T(8,128)(2,1)S(1)}, bf16[4,256,256]{2,1,0:T(8,128)(2,1)S(1)}, u32[]{:S(2)}, u32[]{:S(2)}) collective-permute-start(bf16[4,256,256]{2,1,0:T(8,128)(2,1)S(1)} %get-tuple-element.18), channel_id=1, source_target_pairs={{1,0},{2,1},{3,2},{4,3},{5,4},{6,5},{7,6},{8,7},{9,8},{10,9},{11,1... | collective-permute-start | bytes 1572872 | tf_op jit(solution)/shard_map/ppermute | solution.py:245
  8.2 10.5 %collective-permute-start.1 = (bf16[4,256,256]{2,1,0:T(8,128)(2,1)S(1)}, bf16[4,256,256]{2,1,0:T(8,128)(2,1)S(1)}, u32[]{:S(2)}, u32[]{:S(2)}) collective-permute-start(bf16[4,256,256]{2,1,0:T(8,128)(2,1)S(1)} %get-tuple-element.19), channel_id=1, source_target_pairs={{16,0},{32,16},{48,32},{64,48},{80,64},{96,80},{112,96},{17,1},{33... | collective-permute-start | bytes 1572872 | tf_op jit(solution)/shard_map/ppermute | solution.py:241

commit v4 on v3

--- a/solution.py
+++ b/solution.py
@@ -20,10 +20,13 @@
     return row, col, sub, lax.rem(row, 2)
 
 
-def exchange_order(cols):
+def exchange_orders(cols):
     side = int(cols**0.5)
     y0, z0 = side // 2, side // 2
-    return [(y0 + i + j) % side * side + (z0 + j) % side for i in range(side) for j in range(side)]
+    steps = [(i, j) for i in range(side) for j in range(side)]
+    even = [(y0 + i + j) % side * side + (z0 + j) % side for i, j in steps]
+    odd = [(y0 + i) % side * side + (z0 + i + j) % side for i, j in steps]
+    return even, odd
 
 
 def side_block(owners, lists, direction, first, side, j):
@@ -42,7 +45,7 @@
 
 
 def apply_kernel(
-    nk, cols, groups, index_hbm, owner_hbm, margin_hbm, stiff_hbm, modes_hbm,
+    nk, cols, index_hbm, owner_hbm, margin_hbm, stiff_hbm, modes_hbm,
     total, modes, send_col_ref, send_row_ref,
     index, owners, lists, stiff, small_sem, mode_sem, stiff_sem,
 ):
@@ -51,7 +54,7 @@
         for i, (src, dst) in enumerate(((index_hbm, index), (owner_hbm, owners), (margin_hbm, lists)))
     ]
     mode_copy = pltpu.make_async_copy(modes_hbm, modes, mode_sem)
-    edges = [nk * g // groups for g in range(groups + 1)]
+    edges = [0, nk * 3 // 7, nk]
     stiff_copies = [
         pltpu.make_async_copy(
             stiff_hbm.at[pl.ds(lo, hi - lo)], stiff.at[pl.ds(lo, hi - lo)], stiff_sem.at[g]
@@ -68,7 +71,7 @@
     for copy in small:
         copy.wait()
     mode_copy.wait()
-    for g in range(groups):
+    for g in range(len(stiff_copies)):
         stiff_copies[g].wait()
         for k in range(edges[g], edges[g + 1]):
             product = jnp.dot(stiff[k], modes[index[1, k]], preferred_element_type=F32)
@@ -136,29 +139,28 @@
         fill.wait()
 
 
-def project_kernel(order, diag, keep_col, keep_row, got_col, got_row, pieces):
+def project_kernel(orders, diag, keep_col, keep_row, got_col, got_row, pieces):
     part = pieces.shape[1] // 3
     row_block = jnp.dot(keep_row[...], got_row[...], preferred_element_type=F32).astype(BF16)
     col_block = jnp.dot(keep_col[...], got_col[...], preferred_element_type=F32)
     odd = lax.rem(lax.axis_index("row"), 2)
-    for p, c in enumerate(order):
-        pieces[p, 0:part] = diag[c * part : (c + 1) * part]
-        pieces[p, 2 * part : 3 * part] = row_block[c * part : (c + 1) * part]
-
-    def spread(block):
+
+    def spread(order, column):
         for p, c in enumerate(order):
-            pieces[p, part : 2 * part] = block[c * part : (c + 1) * part]
+            pieces[p, 0:part] = diag[c * part : (c + 1) * part]
+            pieces[p, part : 2 * part] = column[c * part : (c + 1) * part]
+            pieces[p, 2 * part : 3 * part] = row_block[c * part : (c + 1) * part]
 
     @pl.when(odd == 0)
     def _():
-        spread(col_block.astype(BF16))
+        spread(orders[0], col_block.astype(BF16))
 
     @pl.when(odd == 1)
     def _():
-        spread(col_block.T.astype(BF16))
-
-
-def store_kernel(rows, order, received, zeroed, stored, sems):
+        spread(orders[1], col_block.T.astype(BF16))
+
+
+def store_kernel(rows, orders, received, zeroed, stored, sems):
     del zeroed
     cols = received.shape[0]
     part = received.shape[1] // 3
@@ -166,33 +168,32 @@
     odd = lax.rem(row, 2)
     base = row * cols
 
-    def copies(act):
+    def copies(act, parity, order):
         for p, c in enumerate(order):
-            act(pltpu.make_async_copy(received.at[p, 0:part], stored.at[c, base + c], sems.at[0, c]))
-
-            def col_copy(p, local):
+            act(pltpu.make_async_copy(received.at[p, 0:part], stored.at[c, base + c], sems.at[0, p]))
+            first = c - parity
+            if 0 <= first < cols - 1:
                 act(
                     pltpu.make_async_copy(
-                        received.at[p, part : 2 * part], stored.at[local, base + local + 1], sems.at[1, p]
+                        received.at[p, part : 2 * part], stored.at[first, base + first + 1], sems.at[1, p]
                     )
                 )
-
-            if c < cols - 1:
-                pl.when(odd == 0)(functools.partial(col_copy, p, c))
-            if c > 0:
-                pl.when(odd == 1)(functools.partial(col_copy, p, c - 1))
 
         @pl.when(row < rows - 1)
         def _():
             for p, c in enumerate(order):
                 act(
                     pltpu.make_async_copy(
-                        received.at[p, 2 * part : 3 * part], stored.at[c, base + cols + c], sems.at[2, c]
+                        received.at[p, 2 * part : 3 * part], stored.at[c, base + cols + c], sems.at[2, p]
                     )
                 )
 
-    copies(lambda copy: copy.start())
-    copies(lambda copy: copy.wait())
+    for parity, order in enumerate(orders):
+
+        @pl.when(odd == parity)
+        def _():
+            copies(lambda copy: copy.start(), parity, order)
+            copies(lambda copy: copy.wait(), parity, order)
 
 
 def params(mib):
@@ -210,10 +211,9 @@
     index = stiffness_index.T
     owners = pair_owner.T
     lists = margin.transpose(1, 2, 3, 0)
-    groups = 2
     hbm = lambda x: pltpu.with_memory_space_constraint(x, pltpu.HBM)
     total, modes_near, send_col, send_row = pl.pallas_call(
-        functools.partial(apply_kernel, nk, cols, groups),
+        functools.partial(apply_kernel, nk, cols),
         out_shape=(
             pltpu.VMEM((nb, bs, m), F32),
             pltpu.VMEM((nb, bs, m), BF16),
@@ -229,7 +229,7 @@
             pltpu.VMEM((nk, bs, bs), BF16),
             pltpu.SemaphoreType.DMA((3,)),
             pltpu.SemaphoreType.DMA,
-            pltpu.SemaphoreType.DMA((groups,)),
+            pltpu.SemaphoreType.DMA((2,)),
         ],
         compiler_params=params(20),
         cost_estimate=pl.CostEstimate(
@@ -270,9 +270,9 @@
         name="middle",
     )(hbm(owners), hbm(lists), modes_near, total)
 
-    order = exchange_order(cols)
+    orders = exchange_orders(cols)
     pieces = pl.pallas_call(
-        functools.partial(project_kernel, order),
+        functools.partial(project_kernel, orders),
         out_shape=pltpu.VMEM((cols, 3 * part, m), BF16),
         in_specs=[VMEM] * 5,
         out_specs=VMEM,
@@ -284,11 +284,16 @@
     )(diag, keep_col, keep_row, got_col.reshape(ovb * bs, m), got_row.reshape(ovb * bs, m))
 
     received = lax.all_to_all(
-        pieces, "col", split_axis=0, concat_axis=0, axis_index_groups=[order], tiled=True
+        pieces,
+        ("row", "col"),
+        split_axis=0,
+        concat_axis=0,
+        axis_index_groups=[[r * cols + c for c in orders[r % 2]] for r in range(rows)],
+        tiled=True,
     )
 
     return pl.pallas_call(
-        functools.partial(store_kernel, rows, order),
+        functools.partial(store_kernel, rows, orders),
         out_shape=pltpu.HBM(stored.shape, BF16),
         in_specs=[VMEM, HBM],
         out_specs=HBM,

time: 35.3 us -> 35.1 us (level)
  no operation moved by 1% of the time
where the time goes in v4:
time: 35.1 us; the launch traced here: 34.8 us
  blocking collectives  14.5 us (41%)
  Pallas kernels  11.5 us (33%)
  starting transfers between devices  6.31 us (18%)
  waiting for transfers between devices  2.51 us (7%)
    all_to_all x1, blocking collectives, on_device(): lax.all_to_all(pieces, ('row', 'col'), split_axis=0, concat_axis=0, axis_...  14.5 us
    pallas_call x1, Pallas kernels, on_device(): pl.pallas_call(functools.partial(middle_kernel, cols), out_shape=(pltpu.H...  6.05 us
    ppermute x1, starting transfers between devices, on_device(): got_col = lax.ppermute(send_col, ('row', 'col'), line)  4.39 us
    pallas_call x1, Pallas kernels, on_device(): pl.pallas_call(functools.partial(apply_kernel, nk, cols), out_shape=(pltp...  3.7 us
    ppermute x1, waiting for transfers between devices, on_device(): lax.ppermute(send_row, 'row', [(r, r - 1) for r in range(1, rows)])  2.51 us
    ppermute x1, starting transfers between devices, on_device(): lax.ppermute(send_row, 'row', [(r, r - 1) for r in range(1, rows)])  1.92 us
    pallas_call x1, Pallas kernels, on_device(): pl.pallas_call(functools.partial(store_kernel, rows, orders), out_shape=p...  1.2 us
  transfers between devices with their start and end apart: 2, of which 1 were waited for; matrix products, arithmetic and copies ran while one was open for 0% of the time, Pallas kernels for 17%

profile of v4, /device:TPU:1, one launch (start us, length us, event | category | flops | bytes accessed | tf_op | source)
XLA Modules:
  0.0 34.8 jit_solution(5437872254467469713)
XLA Ops:
  0.0 3.7 %apply.1 = (f32[16,256,256]{2,1,0:T(8,128)S(1)}, bf16[16,256,256]{2,1,0:T(8,128)(2,1)S(1)}, bf16[4,256,256]{2,1,0:T(8,128)(2,1)S(1)}, bf16[4,256,256]{2,1,0:T(8,128)(2,1)S(1)}) custom-call(s32[2,28]{1,0:T(2,128)} %bitcast.13, s32[2,128]{1,0:T(2,128)} %bitcast.11, s32[2,4,2,128]{3,2,1,0:T(2,128)} %bitcast.9, bf16[28,256,256]{2,1,0:T(8,128)(2,1)} %stiff_hbm.1, ...), custom_call_target="tpu_custom_call" | custom-call | flops 939524096 | bytes 7864320 | tf_op jit(solution)/shard_map/apply/pallas_call | solution.py:215
  3.7 4.4 %collective-permute-start = (bf16[4,256,256]{2,1,0:T(8,128)(2,1)S(1)}, bf16[4,256,256]{2,1,0:T(8,128)(2,1)S(1)}, u32[]{:S(2)}, u32[]{:S(2)}) collective-permute-start(bf16[4,256,256]{2,1,0:T(8,128)(2,1)S(1)} %get-tuple-element.18), channel_id=1, source_target_pairs={{1,0},{2,1},{3,2},{4,3},{5,4},{6,5},{7,6},{8,7},{9,8},{10,9},{11,1... | collective-permute-start | bytes 1572872 | tf_op jit(solution)/shard_map/ppermute | solution.py:245
  8.1 1.9 %collective-permute-start.1 = (bf16[4,256,256]{2,1,0:T(8,128)(2,1)S(1)}, bf16[4,256,256]{2,1,0:T(8,128)(2,1)S(1)}, u32[]{:S(2)}, u32[]{:S(2)}) collective-permute-start(bf16[4,256,256]{2,1,0:T(8,128)(2,1)S(1)} %get-tuple-element.19), channel_id=1, source_target_pairs={{16,0},{32,16},{48,32},{64,48},{80,64},{96,80},{112,96},{17,1},{33... | collective-permute-start | bytes 1572872 | tf_op jit(solution)/shard_map/ppermute | solution.py:241
  10.0 6.0 %middle.1 = (bf16[16,128,16,256]{3,2,1,0:T(8,128)(2,1)}, bf16[256,256]{1,0:T(8,128)(2,1)S(1)}, bf16[256,1024]{1,0:T(8,128)(2,1)S(1)}, bf16[256,1024]{1,0:T(8,128)(2,1)S(1)}) custom-call(s32[2,128]{1,0:T(2,128)} %bitcast.12, s32[2,4,2,128]{3,2,1,0:T(2,128)} %bitcast.10, bf16[16,256,256]{2,1,0:T(8,128)(2,1)S(1)} %get-tuple-element.13.modes, ...), custom_call_target="tpu_custom_call" | custom-call | flops 536870912 | bytes 16777216 | tf_op jit(solution)/shard_map/middle/pallas_call | solution.py:248
  16.1 0.0 collective-permute-done
  16.1 2.5 %collective-permute-done.1 = bf16[4,256,256]{2,1,0:T(8,128)(2,1)S(1)} collective-permute-done((bf16[4,256,256]{2,1,0:T(8,128)(2,1)S(1)}, bf16[4,256,256]{2,1,0:T(8,128)(2,1)S(1)}, u32[]{:S(2)}, u32[]{:S(2)}) %collective-permute-start.1) | collective-permute-done | bytes 524320 | tf_op jit(solution)/shard_map/ppermute | solution.py:241
  18.6 0.5 %project.1 = bf16[16,48,256]{2,1,0:T(8,128)(2,1)S(1)} custom-call(bf16[256,256]{1,0:T(8,128)(2,1)S(1)} %get-tuple-element.15.diag, bf16[256,1024]{1,0:T(8,128)(2,1)S(1)} %get-tuple-element.16.keep_col, bf16[256,1024]{1,0:T(8,128)(2,1)S(1)} %get-tuple-element.17.keep_row, bf16[1024,256]{1,0:T(8,128)(2,1)S(1)} %bitcast.6, bf16[1024,256]{1,0:T(8,128)(2,1)S(1)} %bitcast.7), custom_call_target="tpu_custom_call" | custom-call | flops 268435456 | bytes 2097152 | tf_op jit(solution)/shard_map/project/pallas_call | solution.py:274
  19.1 14.5 %all_to_all.5.received = bf16[16,48,256]{2,1,0:T(8,128)(2,1)S(1)} all-to-all(bf16[16,48,256]{2,1,0:T(8,128)(2,1)S(1)} %project.1), channel_id=1, replica_groups={{10,15,0,5,14,3,4,9,2,7,8,13,6,11,12,1},{26,27,24,25,31,28,29,30,16,17,..., dimensions={0} | all-to-all | bytes 786432 | tf_op jit(solution)/shard_map/all_to_all | solution.py:286
  33.6 1.2 %store.1 = bf16[16,128,16,256]{3,2,1,0:T(8,128)(2,1)} custom-call(bf16[16,48,256]{2,1,0:T(8,128)(2,1)S(1)} %all_to_all.5.received, bf16[16,128,16,256]{3,2,1,0:T(8,128)(2,1)} %get-tuple-element.20.zeroed), custom_call_target="tpu_custom_call", output_to_operand_aliasing={{}: (1, {})} | custom-call | tf_op jit(solution)/shard_map/store/pallas_call | solution.py:295
Async XLA Ops:
  3.7 12.4 %collective-permute-start = (bf16[4,256,256]{2,1,0:T(8,128)(2,1)S(1)}, bf16[4,256,256]{2,1,0:T(8,128)(2,1)S(1)}, u32[]{:S(2)}, u32[]{:S(2)}) collective-permute-start(bf16[4,256,256]{2,1,0:T(8,128)(2,1)S(1)} %get-tuple-element.18), channel_id=1, source_target_pairs={{1,0},{2,1},{3,2},{4,3},{5,4},{6,5},{7,6},{8,7},{9,8},{10,9},{11,1... | collective-permute-start | bytes 1572872 | tf_op jit(solution)/shard_map/ppermute | solution.py:245
  8.1 10.5 %collective-permute-start.1 = (bf16[4,256,256]{2,1,0:T(8,128)(2,1)S(1)}, bf16[4,256,256]{2,1,0:T(8,128)(2,1)S(1)}, u32[]{:S(2)}, u32[]{:S(2)}) collective-permute-start(bf16[4,256,256]{2,1,0:T(8,128)(2,1)S(1)} %get-tuple-element.19), channel_id=1, source_target_pairs={{16,0},{32,16},{48,32},{64,48},{80,64},{96,80},{112,96},{17,1},{33... | collective-permute-start | bytes 1572872 | tf_op jit(solution)/shard_map/ppermute | solution.py:241
